TPU v7x, 32 devices: a whole 2x2x4 slice. The times are simulated.
32 devices in a mesh: expert: 4 (over x, core), shard: 8 (over z, y).
Axes of the slice: x: 2, y: 2, z: 4, core: 2. Of those that a mesh axis runs over, the one named last changes fastest.
Arguments:
- tokens_in: bfloat16 [1024, 4096], P(('expert', 'shard')), may hold values from -6 to 6
- out_grad: bfloat16 [1024, 2, 8192], P(('expert', 'shard')), may hold values from -6 to 6
- expert_ids: int32 [1024, 2], P(('expert', 'shard')), may hold values from 0 to 3, all different within a row; in each aligned block of 32 rows (0 to 31, 32 to 63, ...) at most 20 rows name the same one
- d_levels: int32 [4, 16], P('expert'), may hold values from 0 to 7
- f_levels: int32 [4, 32], P('expert', 'shard'), may hold values from 0 to 7
Outputs:
- ascent: bfloat16 [4, 4096, 8192], P('expert', None, 'shard')
Inputs may be any that keep to these rules, and one draw needn't show every extreme that they name: `expert_ids`: each token names two different experts; among the 64 entries of one device no expert is named more than 20 times, and 20 is reached on some device; every expert is named somewhere.
All inputs are finite; a program needn't handle non-finite values.
Results may differ from a plain program's by a relative error of at most 0.001.
Values may be sent and summed in bfloat16 or wider, within the bound.
A program may use at most 128 MiB of HBM per device.

v0:
```python
import jax
import jax.numpy as jnp
from jax import lax
from jax.sharding import PartitionSpec as P

BLK = 256


def invert_blocks(blocks):
    lower = jnp.linalg.cholesky(blocks)
    identity = jnp.eye(blocks.shape[-1], dtype=blocks.dtype)
    return jax.vmap(lambda factor: jax.scipy.linalg.cho_solve((factor, True), identity))(lower)


def damping(levels):
    return 0.05 * jnp.exp(0.4 * levels.astype(jnp.float32))


def covariance(rows, levels, row_count):
    blocks = rows.reshape(rows.shape[0], -1, BLK)
    cov = jnp.einsum("rbi,rbj->bij", blocks, blocks, preferred_element_type=jnp.float32) / row_count
    return cov + damping(levels)[:, None, None] * jnp.eye(BLK, dtype=jnp.float32)


def local(tokens_in, out_grad, expert_ids, d_levels, f_levels):
    group_count = lax.axis_size("expert")
    shard_count = lax.axis_size("shard")
    tok_rows = tokens_in.shape[0]
    width = tokens_in.shape[1]
    ff_full = out_grad.shape[2]
    ff_dev = ff_full // shard_count
    capacity = min(tok_rows, max(2, 5 * tok_rows // (2 * group_count)))
    slot_total = group_count * capacity
    flat_ids = expert_ids.reshape(-1)
    member = (flat_ids[:, None] == jnp.arange(group_count, dtype=jnp.int32)[None, :]).astype(
        jnp.int32
    )
    before = jnp.cumsum(member, axis=0) - member
    ranking = jnp.sum(before * member, axis=1)
    target = flat_ids * capacity + ranking
    dispatch = (jnp.arange(slot_total, dtype=jnp.int32)[:, None] == target[None, :]).astype(
        jnp.bfloat16
    )
    per_token = jnp.sum(
        dispatch.reshape(slot_total, tok_rows, 2).astype(jnp.float32), axis=2
    ).astype(jnp.bfloat16)
    x_send = jnp.dot(per_token, tokens_in, preferred_element_type=jnp.float32).astype(jnp.bfloat16)
    g_send = jnp.dot(
        dispatch, out_grad.reshape(2 * tok_rows, ff_full), preferred_element_type=jnp.float32
    ).astype(jnp.bfloat16)
    valid_slot = jnp.sum(dispatch.astype(jnp.float32), axis=1).astype(jnp.bfloat16)
    x_group, g_group, v_group = (
        lax.all_to_all(
            x_send.reshape(group_count, capacity, width),
            "expert",
            split_axis=0,
            concat_axis=1,
            tiled=True,
        ),
        lax.all_to_all(
            g_send.reshape(group_count, capacity, ff_full),
            "expert",
            split_axis=0,
            concat_axis=1,
            tiled=True,
        ),
        lax.all_to_all(
            valid_slot.reshape(group_count, capacity),
            "expert",
            split_axis=0,
            concat_axis=1,
            tiled=True,
        ),
    )
    rows_x, live_rows = (
        lax.all_gather(x_group, "shard", axis=1, tiled=True),
        lax.all_gather(v_group, "shard", axis=1, tiled=True),
    )
    rows_g = lax.all_to_all(g_group, "shard", split_axis=2, concat_axis=1, tiled=True)
    rows_x = rows_x.reshape(-1, width)
    rows_g = rows_g.reshape(-1, ff_dev)
    row_count = jnp.sum(live_rows.astype(jnp.float32))
    gradient = lax.dot_general(
        rows_x, rows_g, (((0,), (0,)), ((), ())), preferred_element_type=jnp.float32
    )
    inv_f = invert_blocks(covariance(rows_g, f_levels[0], row_count))
    grad_blocks = gradient.reshape(width // BLK, BLK, ff_dev)
    highest = lax.Precision.HIGHEST
    own_blocks = width // BLK // shard_count
    first_block = lax.axis_index("shard") * own_blocks
    own_rows = lax.dynamic_slice_in_dim(rows_x, first_block * BLK, own_blocks * BLK, 1)
    own_levels = lax.dynamic_slice_in_dim(d_levels[0], first_block, own_blocks, 0)
    inv_a = invert_blocks(covariance(own_rows, own_levels, row_count))
    left_done = jnp.einsum(
        "bij,bjf->bif",
        lax.all_gather(inv_a, "shard", axis=0, tiled=True),
        grad_blocks,
        precision=highest,
    )
    precond = jnp.einsum(
        "dcj,cjk->dck", left_done.reshape(width, ff_dev // BLK, BLK), inv_f, precision=highest
    ).reshape(width, ff_dev)
    norm_total = lax.psum(jnp.sum(precond * precond), ("expert", "shard"))
    ascent_scale = lax.rsqrt(norm_total / (group_count * width * ff_full) + 1e-06)
    return (precond * ascent_scale).astype(jnp.bfloat16)[None]


def solution(mesh):
    return jax.shard_map(
        local,
        mesh=mesh,
        in_specs=(
            P(("expert", "shard"), None),
            P(("expert", "shard"), None, None),
            P(("expert", "shard"), None),
            P("expert", None),
            P("expert", "shard"),
        ),
        out_specs=P("expert", None, "shard"),
        check_vma=False,
    )
```

profile of v0, /device:TPU:0, one launch (start us, length us, event | category | flops | bytes accessed | tf_op | source)
XLA Modules:
  0.0 676.1 jit_solution(11534804795812444572)
XLA Ops:
  9.3 15.7 %all_to_all.56 = bf16[4,20,4096]{2,1,0:T(8,128)(2,1)S(1)} all-to-all(bf16[4,20,4096]{2,1,0:T(8,128)(2,1)S(1)} %reshape.180), channel_id=1, replica_groups=mesh['expert'=4,'shard'=8] {'expert'}, dimensions={0} | all-to-all | bytes 1310720 | tf_op jit(solution)/shard_map/all_to_all | solution.py:53
  41.6 22.1 %all-reduce.2 = bf16[640]{0:T(1024)(128)(2,1)S(1)} all-reduce(bf16[640]{0:T(1024)(128)(2,1)S(1)} %dynamic-update-slice.22), channel_id=1, replica_groups=mesh['expert'=4,'shard'=8] {'shard'}, use_global_device_ids=true, to_apply=%add.2 | all-reduce | flops 640 | bytes 2560
  64.8 6.8 %copy.134 = bf16[1,80,8192]{1,0,2:T(2,128)(2,1)} copy(bf16[1,80,8192]{2,1,0:T(8,128)(2,1)S(1)} %all_to_all.42) | data formatting | bytes 2621440 | tf_op jit(solution)/shard_map/all_to_all | solution.py:60
  72.1 45.2 %reduce.30 = bf16[8192,80]{1,0:T(8,128)(2,1)S(1)} reduce(bf16[8192,1,80]{2,1,0:T(2,128)(2,1)} %bitcast.114, bf16[]{:T(256)} %broadcast.357), dimensions={1}, to_apply=%bitcast.71.reduce_sub_computation | reduce | bytes 2621442
  129.2 23.5 %custom-call.44 = f32[2,128,128]{2,1,0:T(8,128)S(1)} custom-call(f32[2,128,128]{2,1,0:T(8,128)S(1)} %cholesky.241), custom_call_target="Cholesky" | custom-call | tf_op jit(solution)/shard_map/jit(cholesky)/cholesky | solution.py:10
  153.4 19.7 %custom-call.45 = f32[2,1,128,128]{2,3,1,0:T(8,128)S(1)} custom-call(f32[2,1,128,128]{3,2,1,0:T(8,128)S(1)} %select_bitcast_fusion.1), custom_call_target="InvertDiagBlocksLowerTriangular" | custom-call | tf_op jit(solution)/shard_map/jit(cholesky)/cholesky | solution.py:10
  173.8 23.5 %custom-call.46 = f32[2,128,128]{2,1,0:T(8,128)S(1)} custom-call(f32[2,128,128]{2,1,0:T(8,128)S(1)} %convolution_subtract_fusion.5), custom_call_target="Cholesky" | custom-call | tf_op jit(solution)/shard_map/jit(cholesky)/cholesky | solution.py:10
  199.2 5.3 while.3
  204.5 40.3 %custom-call.47 = f32[2,2,128,128]{2,3,1,0:T(8,128)S(1)} custom-call(f32[2,2,128,128]{3,2,1,0:T(8,128)} %bitcast.125), custom_call_target="InvertDiagBlocksLowerTriangular" | custom-call | tf_op jit(solution)/shard_map/vmap(jit(_cho_solve))/triangular_solve | solution.py:12
  249.1 5.7 reshape.237
  254.8 8.3 %copy.135 = bf16[1,80,8192]{2,1,0:T(8,128)(2,1)S(1)} copy(bf16[1,80,8192]{1,0,2:T(2,128)(2,1)} %bitcast.115) | data formatting | bytes 2621440 | tf_op jit(solution)/shard_map/all_to_all | solution.py:79
  273.5 47.3 %custom-call.40 = f32[4,128,128]{2,1,0:T(8,128)S(1)} custom-call(f32[4,128,128]{2,1,0:T(8,128)S(1)} %cholesky.238), custom_call_target="Cholesky" | custom-call | tf_op jit(solution)/shard_map/jit(cholesky)/cholesky | solution.py:10
  321.0 39.9 %custom-call.41 = f32[4,1,128,128]{2,3,1,0:T(8,128)} custom-call(f32[4,1,128,128]{3,2,1,0:T(8,128)S(1)} %select_bitcast_fusion), custom_call_target="InvertDiagBlocksLowerTriangular" | custom-call | tf_op jit(solution)/shard_map/jit(cholesky)/cholesky | solution.py:10
  364.7 47.7 %custom-call.42 = f32[4,128,128]{2,1,0:T(8,128)S(1)} custom-call(f32[4,128,128]{2,1,0:T(8,128)} %convolution_subtract_fusion.4), custom_call_target="Cholesky" | custom-call | tf_op jit(solution)/shard_map/jit(cholesky)/cholesky | solution.py:10
  414.9 5.3 while.2
  420.2 79.6 %custom-call.43 = f32[4,2,128,128]{2,3,1,0:T(8,128)S(1)} custom-call(f32[4,2,128,128]{3,2,1,0:T(8,128)} %bitcast.124), custom_call_target="InvertDiagBlocksLowerTriangular" | custom-call | tf_op jit(solution)/shard_map/vmap(jit(_cho_solve))/triangular_solve | solution.py:12
  505.4 7.8 %copy.157 = bf16[4096,640]{1,0:T(8,128)(2,1)} copy(bf16[4096,640]{0,1:T(8,128)(2,1)} %bitcast.116) | data formatting | bytes 10485760 | tf_op jit(solution)/shard_map/dot_general | solution.py:83
  513.3 12.7 %fusion.41 = f32[16,256,1024]{2,1,0:T(8,128)} fusion(bf16[16,256,640]{2,1,0:T(8,128)(2,1)} %bitcast.117, bf16[640,1024,1]{1,0,2:T(8,128)(2,1)S(1)} %bitcast.118), kind=kOutput, calls=%fused_computation.98 | convolution fusion | flops 5368709120 | bytes 23330816 | tf_op jit(solution)/shard_map/dot_general | solution.py:83
  525.9 22.9 %fusion.42 = f32[16,256,1024]{2,1,0:T(8,128)} fusion(f32[16,256,256]{2,1,0:T(8,128)} %all-gather.5.cloned.1.call-done, f32[16,256,1024]{2,1,0:T(8,128)} %fusion.41), kind=kOutput, calls=%fused_computation.99 | convolution fusion | flops 12884901888 | bytes 37748736 | tf_op jit(solution)/shard_map/bij,bjf->bif/dot_general | solution.py:94
  548.8 20.4 %reshape.184 = f32[4096,4,256]{2,1,0:T(4,128)} reshape(f32[16,256,1024]{2,1,0:T(8,128)} %fusion.42) | data formatting | bytes 33554432 | tf_op jit(solution)/shard_map/reshape | solution.py:101
  569.2 36.8 %multiply_reduce_fusion = (f32[]{:T(128)}, f32[4,256,4096]{2,1,0:T(8,128)}) fusion(f32[4096,4,256]{2,1,0:T(4,128)} %reshape.184, f32[4,128,256]{2,1,0:T(8,128)S(1)} %fusion.14, f32[4,128,256]{2,1,0:T(8,128)S(1)} %fusion.13), kind=kOutput, calls=%fused_computation.7 | convolution fusion | flops 12893552640 | bytes 34603012 | tf_op jit(solution)/shard_map/dcj,cjk->dck/dot_general | solution.py:100
  606.0 41.1 %psum.7 = f32[]{:T(128)} all-reduce(f32[]{:T(128)} %get-tuple-element.53), channel_id=1, replica_groups=mesh['expert'=4,'shard'=8] {'expert','shard'}, use_global_device_ids=true, to_apply=%region_14.15 | all-reduce | flops 1 | bytes 8 | tf_op jit(solution)/shard_map/psum | solution.py:103
  647.8 9.1 %multiply_convert_fusion = bf16[4,256,4096]{2,1,0:T(8,128)(2,1)} fusion(f32[4,256,4096]{2,1,0:T(8,128)} %get-tuple-element.54, f32[]{:T(128)S(6)} %rsqrt.3), kind=kLoop, calls=%fused_computation.6 | loop fusion | flops 8388608 | bytes 25165828 | tf_op jit(solution)/shard_map/convert_element_type | solution.py:105
  656.9 12.0 %copy.161 = bf16[1,4096,1024]{2,1,0:T(8,128)(2,1)} copy(bf16[1,4096,1024]{1,2,0:T(8,128)(2,1)} %bitcast.113) | data formatting | bytes 16777216 | tf_op jit(solution)/shard_map/convert_element_type | solution.py:105
  (129 shorter events, 72.4 us)
Async XLA Ops:
  6.5 2.2 copy-start
  6.5 119.2 %all-gather.3.cloned.1.call-start = ((), (), s32[]{:S(2)}) async-start(), calls=%async_computation.4 | async-start | bytes 5898240 | tf_op jit(solution)/shard_map/all_gather | solution.py:76
  25.9 7.4 %copy-start.10 = (u32[32]{0:T(128)S(1)}, u32[32]{0:T(128)}, u32[]{:S(2)}) copy-start(u32[32]{0:T(128)} %constant.263) | copy-start | bytes 388
  26.8 7.9 %all-to-all-start.2 = ((bf16[4,1,20]{2,1,0:T(2,128)(2,1)}), bf16[4,1,20]{2,1,0:T(2,128)(2,1)S(1)}, u32[]{:S(2)}, u32[]{:S(2)}) async-start(bf16[4,1,20]{2,1,0:T(2,128)(2,1)} %all_to_all.51), calls=%async_computation.2 | async-start | bytes 4096 | tf_op jit(solution)/shard_map/all_to_all | solution.py:67
  31.4 7.3 %copy-start.8 = (s32[1,16]{1,0:T(1,128)S(1)}, s32[1,16]{1,0:T(1,128)}, u32[]{:S(2)}) copy-start(s32[1,16]{1,0:T(1,128)} %param.8) | copy-start | bytes 196
  34.7 29.8 %all-to-all-start = ((bf16[4,20,8192]{2,1,0:T(8,128)(2,1)}), bf16[4,20,8192]{2,1,0:T(8,128)(2,1)S(1)}, u32[]{:S(2)}, u32[]{:S(2)}) async-start(bf16[4,20,8192]{2,1,0:T(8,128)(2,1)} %reshape.179), calls=%async_computation | async-start | bytes 3145728 | tf_op jit(solution)/shard_map/all_to_all | solution.py:60
  121.9 127.1 %all-to-all-start.1 = ((bf16[8,2,40960]{2,1,0:T(2,128)(2,1)}), bf16[8,2,40960]{2,1,0:T(2,128)(2,1)S(1)}, u32[]{:S(2)}, u32[]{:S(2)}) async-start(bf16[8,2,40960]{2,1,0:T(2,128)(2,1)} %reshape.236), calls=%async_computation.1 | async-start | bytes 2621440 | tf_op jit(solution)/shard_map/all_to_all | solution.py:79
  125.5 400.4 %all-gather.5.cloned.1.call-start = ((), (), s32[]{:S(2)}) async-start(), calls=%async_computation.5 | async-start | bytes 4718592 | tf_op jit(solution)/shard_map/all_gather | solution.py:96
  197.6 51.5 %copy-start.9 = (s32[1,4]{1,0:T(1,128)S(1)}, s32[1,4]{1,0:T(1,128)}, u32[]{:S(2)}) copy-start(s32[1,4]{1,0:T(1,128)} %param.9) | copy-start | bytes 52
  269.7 51.2 %copy-start.7 = (pred[128,128]{1,0:T(8,128)(4,1)S(1)}, pred[128,128]{1,0:T(8,128)(4,1)}, u32[]{:S(2)}) copy-start(pred[128,128]{1,0:T(8,128)(4,1)} %iota_compare_fusion.3) | copy-start | bytes 49156
  271.0 142.4 %copy-start.6 = (pred[256,256]{1,0:T(8,128)(4,1)S(1)}, pred[256,256]{1,0:T(8,128)(4,1)}, u32[]{:S(2)}) copy-start(pred[256,256]{1,0:T(8,128)(4,1)} %iota_compare_fusion.2) | copy-start | bytes 196612
  272.5 1.0 copy-start.3
  360.9 139.5 %copy-start.5 = (f32[128,256]{1,0:T(8,128)S(1)}, f32[128,256]{1,0:T(8,128)}, u32[]{:S(2)}) copy-start(f32[128,256]{1,0:T(8,128)} %get-tuple-element.46) | copy-start | bytes 393220
  412.5 1.0 copy-start.2
  499.8 1.2 copy-start.4
  656.9 12.0 %copy-start.1 = (bf16[32,4096]{1,0:T(8,128)(2,1)S(1)}, bf16[32,4096]{1,0:T(8,128)(2,1)}, u32[]{:S(2)}) copy-start(bf16[32,4096]{1,0:T(8,128)(2,1)} %param.5) | copy-start | bytes 786436
Sparse Core Ops, SparseCore 0:
  26.1 86.4 all-gather.2
  249.1 74.5 all-gather.4
where the time goes:
time: 686 us; the launch traced here: 676 us
  other arithmetic  387 us (56%)
  local copies, waits for them, and re-layouts  93.3 us (14%)
  matrix products  90.7 us (13%)
  blocking collectives  79 us (12%)
  between operations  15.7 us (2%)
  starting transfers between devices  10.5 us (2%)
    another operation x18, other arithmetic, invert_blocks(): lower = jnp.linalg.cholesky(blocks)  203 us
    another operation x7, other arithmetic, invert_blocks(): jax.scipy.linalg.cho_solve((factor, True), identity)  124 us
    unnamed x3, other arithmetic  45.2 us
    psum x1, blocking collectives, local(): norm_total = lax.psum(jnp.sum(precond * precond), ('expert', 'shard'))  41.1 us
    dot_general x1, matrix products, local(): jnp.einsum('dcj,cjk->dck', left_done.reshape(width, ff_dev // BLK, BLK),...  36.8 us
    dot_general x1, matrix products, local(): jnp.einsum('bij,bjf->bif', lax.all_gather(inv_a, 'shard', axis=0, tiled=T...  22.9 us
    unnamed x1, blocking collectives  22.1 us
    reshape x1, local copies, waits for them, and re-layouts, local(): left_done.reshape(width, ff_dev // BLK, BLK)  20.4 us
  transfers between devices with their start and end apart: 5, of which 0 were waited for; matrix products, arithmetic and copies ran while one was open for 69% of the time, Pallas kernels for 0%

commit v1 on v0

v1 whole, which is shorter than its diff:
```python
import functools

import jax
import jax.numpy as jnp
from jax import lax
from jax.experimental import pallas as pl
from jax.experimental.pallas import tpu as pltpu
from jax.sharding import PartitionSpec as P

BLK = 256
HALF = BLK // 2
MARK = 128
NT = (((1,), (1,)), ((), ()))
TN = (((0,), (0,)), ((), ()))


def dot_f32(a, b, dims=(((1,), (0,)), ((), ()))):
    return lax.dot_general(
        a, b, dims, precision=lax.Precision.HIGHEST, preferred_element_type=jnp.float32
    )


def dot_bf16(a, b, dims=(((1,), (0,)), ((), ()))):
    return lax.dot_general(a, b, dims, preferred_element_type=jnp.float32)


def split(value, parts):
    out = []
    for _ in range(parts):
        part = value.astype(jnp.bfloat16)
        out.append(part)
        value = value - part.astype(jnp.float32)
    return out


def gauss_jordan(work, count):
    lanes = lax.broadcasted_iota(jnp.int32, (HALF, HALF), 1)
    lane_row = lax.broadcasted_iota(jnp.int32, (1, HALF), 1)

    def step(j, carry):
        index = jnp.full((HALF, HALF), j, jnp.int32)
        at_pivot = lanes == j
        for b in range(count):
            matrix = work[b]
            row = work[b, pl.ds(j, 1), :]
            column = jnp.take_along_axis(matrix, index, axis=1)
            pivot = jnp.sum(jnp.where(lane_row == j, row, 0.0), axis=1, keepdims=True)
            scaled = jnp.where(lane_row == j, 1.0, row) / pivot
            work[b] = jnp.where(at_pivot, 0.0, matrix) - column * scaled
            work[b, pl.ds(j, 1), :] = scaled
        return carry

    lax.fori_loop(0, HALF, step, 0)


def invert_covariances(rows_ref, damp_ref, count_ref, work, cov, aux):
    count = cov.shape[0]
    eye = (
        lax.broadcasted_iota(jnp.int32, (BLK, BLK), 0)
        == lax.broadcasted_iota(jnp.int32, (BLK, BLK), 1)
    )
    for b in range(count):
        rows = rows_ref[:, b * BLK : (b + 1) * BLK]
        product = dot_bf16(rows, rows, TN) / count_ref[0]
        cov[b] = product + jnp.where(eye, damp_ref[b], 0.0)
        work[b] = cov[b, :HALF, :HALF]
    gauss_jordan(work, count)
    for b in range(count):
        first = work[b]
        upper = cov[b, :HALF, HALF:]
        side = dot_f32(first, upper)
        aux[b] = side
        cov[b, :HALF, :HALF] = first
        work[b] = cov[b, HALF:, HALF:] - dot_f32(upper, side, TN)
    gauss_jordan(work, count)
    for b in range(count):
        last = work[b]
        side = aux[b]
        corner = dot_f32(side, last)
        cov[b, :HALF, :HALF] = cov[b, :HALF, :HALF] + dot_f32(corner, side, NT)
        cov[b, :HALF, HALF:] = -corner
        cov[b, HALF:, :HALF] = -corner.T
        cov[b, HALF:, HALF:] = last


def input_kernel(damp_ref, count_ref, rows_ref, inv_ref, work, aux):
    invert_covariances(rows_ref, damp_ref, count_ref, work, inv_ref, aux)


def hidden_kernel(damp_ref, count_ref, rows_ref, high_ref, low_ref, work, aux, cov):
    invert_covariances(rows_ref, damp_ref, count_ref, work, cov, aux)
    for b in range(cov.shape[0]):
        columns = slice(b * BLK, (b + 1) * BLK)
        rows = rows_ref[:, columns]
        total = sum(dot_bf16(rows, part) for part in reversed(split(cov[b], 3)))
        high_ref[:, columns], low_ref[:, columns] = split(total, 2)


def product_kernel(rows_ref, inv_ref, high_ref, low_ref, out_ref, norm_ref):
    rows = rows_ref[0]
    left = sum(dot_bf16(part, rows, NT) for part in reversed(split(inv_ref[0], 3)))
    left_high, left_low = split(left, 2)
    high = high_ref[...]
    out = dot_bf16(left_high, low_ref[...]) + dot_bf16(left_low, high) + dot_bf16(left_high, high)
    out_ref[...] = out

    @pl.when(pl.program_id(0) == 0)
    def _():
        norm_ref[...] = jnp.zeros_like(norm_ref)

    norm_ref[...] += jnp.sum((out * out).reshape(-1, 8, out.shape[1]), axis=0)


def damping(levels):
    return 0.05 * jnp.exp(0.4 * levels.astype(jnp.float32))


def call_blocks(kernel, damp, row_count, rows, out_shape, with_cov):
    count = damp.shape[0]
    scratch = [pltpu.VMEM((count, HALF, HALF), jnp.float32)] * 2
    if with_cov:
        scratch.append(pltpu.VMEM((count, BLK, BLK), jnp.float32))
    vmem = pl.BlockSpec(memory_space=pltpu.VMEM)
    smem = pl.BlockSpec(memory_space=pltpu.SMEM)
    return pl.pallas_call(
        kernel,
        out_shape=out_shape,
        in_specs=[smem, smem, vmem],
        out_specs=jax.tree.map(lambda _: vmem, out_shape),
        scratch_shapes=scratch,
        compiler_params=pltpu.CompilerParams(vmem_limit_bytes=48 << 20),
        cost_estimate=pl.CostEstimate(flops=20_000_000_000, bytes_accessed=4_000_000, transcendentals=0),
    )(damp, row_count, rows)


def local(tokens_in, out_grad, expert_ids, d_levels, f_levels):
    group_count = lax.axis_size("expert")
    shard_count = lax.axis_size("shard")
    tok_rows = tokens_in.shape[0]
    width = tokens_in.shape[1]
    ff_full = out_grad.shape[2]
    ff_dev = ff_full // shard_count
    width_dev = width // shard_count
    capacity = min(tok_rows, max(2, 5 * tok_rows // (2 * group_count)))
    slot_total = group_count * capacity
    flat_ids = expert_ids.reshape(-1)
    member = (flat_ids[:, None] == jnp.arange(group_count, dtype=jnp.int32)[None, :]).astype(
        jnp.int32
    )
    before = jnp.cumsum(member, axis=0) - member
    ranking = jnp.sum(before * member, axis=1)
    target = flat_ids * capacity + ranking
    dispatch = (jnp.arange(slot_total, dtype=jnp.int32)[:, None] == target[None, :]).astype(
        jnp.bfloat16
    )
    per_token = jnp.sum(
        dispatch.reshape(slot_total, tok_rows, 2).astype(jnp.float32), axis=2
    ).astype(jnp.bfloat16)
    x_send = jnp.dot(per_token, tokens_in, preferred_element_type=jnp.float32).astype(jnp.bfloat16)
    g_send = jnp.dot(
        dispatch, out_grad.reshape(2 * tok_rows, ff_full), preferred_element_type=jnp.float32
    ).astype(jnp.bfloat16)
    valid_slot = jnp.sum(dispatch.astype(jnp.float32), axis=1).astype(jnp.bfloat16)
    send = jnp.concatenate(
        (
            x_send.reshape(group_count, capacity, shard_count, width_dev),
            g_send.reshape(group_count, capacity, shard_count, ff_dev),
            jnp.broadcast_to(
                valid_slot.reshape(group_count, capacity, 1, 1),
                (group_count, capacity, shard_count, MARK),
            ),
        ),
        axis=3,
    )
    send = send.transpose(0, 2, 1, 3).reshape(group_count * shard_count, capacity, -1)
    rows = lax.all_to_all(send, ("expert", "shard"), split_axis=0, concat_axis=0, tiled=True)
    rows = rows.reshape(-1, rows.shape[2])
    own_x = rows[:, :width_dev]
    rows_g = rows[:, width_dev : width_dev + ff_dev]
    row_count = jnp.sum(rows[:, width_dev + ff_dev].astype(jnp.float32)).reshape(1)
    row_total = rows.shape[0]
    rows_x = lax.all_gather(own_x, "shard", axis=0)

    own_blocks = width_dev // BLK
    first_block = lax.axis_index("shard") * own_blocks
    own_levels = lax.dynamic_slice_in_dim(d_levels[0], first_block, own_blocks, 0)
    inv_a = call_blocks(
        input_kernel,
        damping(own_levels),
        row_count,
        own_x,
        jax.ShapeDtypeStruct((own_blocks, BLK, BLK), jnp.float32),
        False,
    )
    inv_a = lax.all_gather(inv_a, "shard", axis=0, tiled=True)
    half = jax.ShapeDtypeStruct((row_total, ff_dev), jnp.bfloat16)
    g_high, g_low = call_blocks(
        hidden_kernel, damping(f_levels[0]), row_count, rows_g, (half, half), True
    )
    blocks = width // BLK
    whole = pl.BlockSpec((row_total, ff_dev), lambda b: (0, 0))
    precond, squares = pl.pallas_call(
        product_kernel,
        grid=(blocks,),
        out_shape=(
            jax.ShapeDtypeStruct((width, ff_dev), jnp.float32),
            jax.ShapeDtypeStruct((8, ff_dev), jnp.float32),
        ),
        in_specs=[
            pl.BlockSpec((1, row_total, BLK), lambda b: (b // own_blocks, 0, b % own_blocks)),
            pl.BlockSpec((1, BLK, BLK), lambda b: (b, 0, 0)),
            whole,
            whole,
        ],
        out_specs=(
            pl.BlockSpec((BLK, ff_dev), lambda b: (b, 0)),
            pl.BlockSpec((8, ff_dev), lambda b: (0, 0)),
        ),
        compiler_params=pltpu.CompilerParams(
            dimension_semantics=("arbitrary",), vmem_limit_bytes=48 << 20
        ),
        cost_estimate=pl.CostEstimate(
            flops=6 * row_total * width * ff_dev, bytes_accessed=4 * width * ff_dev, transcendentals=0
        ),
    )(rows_x, inv_a, g_high, g_low)
    norm_total = lax.psum(jnp.sum(squares), ("expert", "shard"))
    ascent_scale = lax.rsqrt(norm_total / (group_count * width * ff_full) + 1e-06)
    return (precond * ascent_scale).astype(jnp.bfloat16)[None]


def solution(mesh):
    return jax.shard_map(
        local,
        mesh=mesh,
        in_specs=(
            P(("expert", "shard"), None),
            P(("expert", "shard"), None, None),
            P(("expert", "shard"), None),
            P("expert", None),
            P("expert", "shard"),
        ),
        out_specs=P("expert", None, "shard"),
        check_vma=False,
    )
```

time: 686 us -> 393 us (0.57); the launches traced: 676 us -> 392 us
  other arithmetic: 387 us -> 13.4 us
  Pallas kernels: 0 us -> 211 us
  waiting for transfers between devices: 0.06 us -> 97.8 us
  matrix products: 90.7 us -> 0.95 us
  local copies, waits for them, and re-layouts: 93.3 us -> 9.13 us
  blocking collectives: 79 us -> 38.8 us
    another operation x25 -> x0, other arithmetic: 328 us -> none  [the longest x18 203 us: invert_blocks(): lower = jnp.linalg.cholesky(blocks)]
    pallas_call x0 -> x3, Pallas kernels: none -> 211 us  [the longest x2 179 us: call_blocks(): pl.pallas_call(kernel, out_shape=out_shape, in_specs=[smem, smem, vmem],...]
    dot_general x5 -> x0, matrix products: 76.4 us -> none  [the longest x1 36.8 us: local(): jnp.einsum('dcj,cjk->dck', left_done.reshape(width, ff_dev // BLK, BLK),...]
    all_to_all x3 -> x1, waiting for transfers between devices: 0.01 us -> 59.9 us  [local(): lax.all_to_all(send, ('expert', 'shard'), split_axis=0, concat_axis=0, ti...]
    unnamed x3 -> x0, other arithmetic: 45.2 us -> none
    all_gather x2, waiting for transfers between devices: 0.02 us -> 37.1 us  [the longest x1 37.1 us: local(): rows_x = lax.all_gather(own_x, 'shard', axis=0)]
    unnamed x1 -> x0, blocking collectives: 22.1 us -> none
    reshape x4 -> x1, local copies, waits for them, and re-layouts: 22 us -> 1.99 us  [local(): rows = rows.reshape(-1, rows.shape[2])]
  transfers between devices with their start and end apart: 5 -> 3, of which waited for: 0 -> 2; matrix products, arithmetic and copies ran while one was open for 69% -> 0% of each run, Pallas kernels for 0% -> 30%
where the time goes in v1:
time: 393 us; the launch traced here: 392 us
  Pallas kernels  211 us (54%)
  waiting for transfers between devices  97.8 us (25%)
  blocking collectives  38.8 us (10%)
  between operations  14.3 us (4%)
  other arithmetic  13.4 us (3%)
  local copies, waits for them, and re-layouts  9.13 us (2%)
  starting transfers between devices  7.41 us (2%)
    pallas_call x2, Pallas kernels, call_blocks(): pl.pallas_call(kernel, out_shape=out_shape, in_specs=[smem, smem, vmem],...  179 us
    all_to_all x1, waiting for transfers between devices, local(): lax.all_to_all(send, ('expert', 'shard'), split_axis=0, concat_axis=0, ti...  59.9 us
    psum x1, blocking collectives, local(): norm_total = lax.psum(jnp.sum(squares), ('expert', 'shard'))  38.8 us
    all_gather x1, waiting for transfers between devices, local(): rows_x = lax.all_gather(own_x, 'shard', axis=0)  37.1 us
    pallas_call x1, Pallas kernels, local(): pl.pallas_call(product_kernel, grid=(blocks,), out_shape=(jax.ShapeDtypeS...  31.5 us
    broadcast_in_dim x1, other arithmetic, local(): return (precond * ascent_scale).astype(jnp.bfloat16)[None]  9.6 us
  transfers between devices with their start and end apart: 3, of which 2 were waited for; matrix products, arithmetic and copies ran while one was open for 0% of the time, Pallas kernels for 30%

profile of v1, /device:TPU:0, one launch (start us, length us, event | category | flops | bytes accessed | tf_op | source)
XLA Modules:
  0.0 392.2 jit_solution(892232452843853915)
XLA Ops:
  6.5 0.9 copy.23
  7.7 0.2 select_reduce_fusion
  8.2 0.7 multiply_add_fusion
  9.0 0.3 convolution_convert_fusion.1
  9.4 0.2 copy.26
  9.6 0.4 reshape.55
  10.1 0.6 convolution_convert_fusion
  10.7 0.8 copy.27
  11.6 0.2 maximum_bitcast_fusion
  11.8 1.8 copy.25
  13.6 7.3 %all-to-all-start = ((bf16[32,20,1664]{2,1,0:T(8,128)(2,1)}), bf16[32,20,1664]{2,1,0:T(8,128)(2,1)S(1)}, u32[]{:S(2)}, u32[]{:S(2)}) async-start(bf16[32,20,1664]{2,1,0:T(8,128)(2,1)} %bitcast.20), calls=%async_computation | async-start | bytes 5111808 | tf_op jit(solution)/shard_map/all_to_all | solution.py:176
  21.0 59.9 %all-to-all-done = bf16[32,20,1664]{2,1,0:T(8,128)(2,1)S(1)} async-done(((bf16[32,20,1664]{2,1,0:T(8,128)(2,1)}), bf16[32,20,1664]{2,1,0:T(8,128)(2,1)S(1)}, u32[]{:S(2)}, u32[]{:S(2)}) %all-to-all-start) | async-done | bytes 2129952 | tf_op jit(solution)/shard_map/all_to_all | solution.py:176
  81.0 2.0 reshape.58
  82.9 1.7 convert_reduce_fusion
  84.6 1.1 slice.12.rows_ref
  85.8 60.7 %shard_map.55 = f32[2,256,256]{2,1,0:T(8,128)} custom-call(f32[2]{0:T(128)S(1)} %multiply_bitcast_fusion.1.damp_ref, f32[1]{0:T(128)} %bitcast.4.count_ref, bf16[640,512]{1,0:T(8,128)(2,1)S(1)} %slice.12.rows_ref), custom_call_target="tpu_custom_call" | custom-call | flops 20000000000 | bytes 4000000 | tf_op jit(solution)/shard_map/pallas_call | solution.py:125
  146.5 0.7 all-gather.6.cloned.1.call-update
  147.3 1.4 slice.14.rows_ref
  148.7 118.4 %shard_map.56 = (bf16[640,1024]{1,0:T(8,128)(2,1)S(1)}, bf16[640,1024]{1,0:T(8,128)(2,1)S(1)}) custom-call(f32[4]{0:T(128)S(1)} %multiply_bitcast_fusion.damp_ref, f32[1]{0:T(128)} %bitcast.4.count_ref, bf16[640,1024]{1,0:T(8,128)(2,1)S(1)} %slice.14.rows_ref), custom_call_target="tpu_custom_call" | custom-call | flops 20000000000 | bytes 4000000 | tf_op jit(solution)/shard_map/pallas_call | solution.py:125
  267.1 37.1 %all-gather.6.cloned.1.call-done = bf16[5120,512]{1,0:T(8,128)(2,1)} async-done(((bf16[640,512]{1,0:T(8,128)(2,1)}), bf16[5120,512]{1,0:T(8,128)(2,1)}) %all-gather.6.cloned.1.call-update) | async-done | bytes 5242896 | tf_op jit(solution)/shard_map/all_gather | solution.py:182
  304.2 31.5 %shard_map.57 = (f32[4096,1024]{1,0:T(8,128)}, f32[8,1024]{1,0:T(8,128)S(1)}) custom-call(bf16[8,640,512]{2,1,0:T(8,128)(2,1)} %bitcast.25, f32[16,256,256]{2,1,0:T(8,128)} %all-gather.4.cloned.1.call-done.inv_ref, bf16[640,1024]{1,0:T(8,128)(2,1)S(1)} %get-tuple-element.9.high_ref, bf16[640,1024]{1,0:T(8,128)(2,1)S(1)} %get-tuple-element.10.low_ref), custom_call_target="tpu_custom_call" | custom-call | flops 16106127360 | bytes 16777216 | tf_op jit(solution)/shard_map/pallas_call | solution.py:202
  335.7 0.6 reduce_sum.58
  336.3 38.8 %psum.7 = f32[]{:T(128)} all-reduce(f32[]{:T(128)} %reduce_sum.58), channel_id=1, replica_groups=mesh['expert'=4,'shard'=8] {'expert','shard'}, use_global_device_ids=true, to_apply=%region_6.7 | all-reduce | flops 1 | bytes 8 | tf_op jit(solution)/shard_map/psum | solution.py:226
  375.8 9.6 %fusion = bf16[1,4096,1024]{2,1,0:T(8,128)(2,1)} fusion(f32[4096,1024]{1,0:T(8,128)} %get-tuple-element.11, f32[]{:T(128)S(6)} %rsqrt.3), kind=kLoop, calls=%fused_computation.2 | loop fusion | flops 8388608 | bytes 25165828 | tf_op jit(solution)/shard_map/broadcast_in_dim | solution.py:228
  (26 shorter events, 1.1 us)
Async XLA Ops:
  6.5 2.5 copy-start
  6.5 3.1 copy-start.2
  13.6 7.4 %copy-start.3 = (s32[1,16]{1,0:T(1,128)S(1)}, s32[1,16]{1,0:T(1,128)}, u32[]{:S(2)}) copy-start(s32[1,16]{1,0:T(1,128)} %param.8) | copy-start | bytes 196
  13.6 67.4 %all-to-all-start = ((bf16[32,20,1664]{2,1,0:T(8,128)(2,1)}), bf16[32,20,1664]{2,1,0:T(8,128)(2,1)S(1)}, u32[]{:S(2)}, u32[]{:S(2)}) async-start(bf16[32,20,1664]{2,1,0:T(8,128)(2,1)} %bitcast.20), calls=%async_computation | async-start | bytes 5111808 | tf_op jit(solution)/shard_map/all_to_all | solution.py:176
  20.9 246.2 %all-gather.4.cloned.1.call-start = ((), (), s32[]{:S(2)}) async-start(), calls=%async_computation.1 | async-start | bytes 4718592 | tf_op jit(solution)/shard_map/all_gather | solution.py:195
  85.7 60.7 %copy-start.1 = (bf16[640,512]{1,0:T(8,128)(2,1)}, bf16[640,512]{1,0:T(8,128)(2,1)S(1)}, u32[]{:S(2)}) copy-start(bf16[640,512]{1,0:T(8,128)(2,1)S(1)} %slice.12.rows_ref) | copy-start | bytes 1966084
  85.8 61.5 %copy-start.4 = (s32[1,4]{1,0:T(1,128)S(1)}, s32[1,4]{1,0:T(1,128)}, u32[]{:S(2)}) copy-start(s32[1,4]{1,0:T(1,128)} %param.9) | copy-start | bytes 52
  146.5 157.7 %all-gather.6.cloned.1.call-start = ((), (), s32[]{:S(2)}) async-start(), calls=%async_computation.2 | async-start | bytes 5898240 | tf_op jit(solution)/shard_map/all_gather | solution.py:182
Sparse Core Ops, SparseCore 0:
  146.6 70.5 all-gather.3
  219.4 84.7 all-gather.5

commit v2 on v1

--- a/solution.py
+++ b/solution.py
@@ -40,14 +40,23 @@
     def step(j, carry):
         index = jnp.full((HALF, HALF), j, jnp.int32)
         at_pivot = lanes == j
+        matrices = [work[b] for b in range(count)]
+        rows = [work[b, pl.ds(j, 1), :] for b in range(count)]
+        pivots = [
+            jnp.sum(jnp.where(lane_row == j, row, 0.0), axis=1, keepdims=True) for row in rows
+        ]
+        columns = [jnp.take_along_axis(matrix, index, axis=1) for matrix in matrices]
+        scaled = [
+            jnp.where(lane_row == j, 1.0, row) / pivot for row, pivot in zip(rows, pivots)
+        ]
+        updated = [
+            jnp.where(at_pivot, 0.0, matrix) - column * row
+            for matrix, column, row in zip(matrices, columns, scaled)
+        ]
         for b in range(count):
-            matrix = work[b]
-            row = work[b, pl.ds(j, 1), :]
-            column = jnp.take_along_axis(matrix, index, axis=1)
-            pivot = jnp.sum(jnp.where(lane_row == j, row, 0.0), axis=1, keepdims=True)
-            scaled = jnp.where(lane_row == j, 1.0, row) / pivot
-            work[b] = jnp.where(at_pivot, 0.0, matrix) - column * scaled
-            work[b, pl.ds(j, 1), :] = scaled
+            work[b] = updated[b]
+        for b in range(count):
+            work[b, pl.ds(j, 1), :] = scaled[b]
         return carry
 
     lax.fori_loop(0, HALF, step, 0)

time: 393 us -> 371 us (0.944)
  Pallas kernels: 211 us -> 124 us
  waiting for transfers between devices: 97.8 us -> 164 us
    pallas_call x2, Pallas kernels: 179 us -> 92.2 us  [call_blocks(): pl.pallas_call(kernel, out_shape=out_shape, in_specs=[smem, smem, vmem],...]
    all_gather x1, waiting for transfers between devices: 37.1 us -> 86.6 us  [local(): rows_x = lax.all_gather(own_x, 'shard', axis=0)]
    all_gather x1, waiting for transfers between devices: 0.02 us -> 16.4 us  [local(): inv_a = lax.all_gather(inv_a, 'shard', axis=0, tiled=True)]
  transfers between devices with their start and end apart: 3 -> 3, of which waited for: 2 -> 3; matrix products, arithmetic and copies ran while one was open for 0% -> 0% of each run, Pallas kernels for 30% -> 14%
where the time goes in v2:
time: 371 us
  waiting for transfers between devices  164 us (44%)
  Pallas kernels  124 us (33%)
  blocking collectives  38.6 us (10%)
  between operations  14.3 us (4%)
  other arithmetic  13.4 us (4%)
  local copies, waits for them, and re-layouts  9.13 us (2%)
  starting transfers between devices  7.41 us (2%)
    pallas_call x2, Pallas kernels, call_blocks(): pl.pallas_call(kernel, out_shape=out_shape, in_specs=[smem, smem, vmem],...  92.2 us
    all_gather x1, waiting for transfers between devices, local(): rows_x = lax.all_gather(own_x, 'shard', axis=0)  86.6 us
    all_to_all x1, waiting for transfers between devices, local(): lax.all_to_all(send, ('expert', 'shard'), split_axis=0, concat_axis=0, ti...  59.9 us
    psum x1, blocking collectives, local(): norm_total = lax.psum(jnp.sum(squares), ('expert', 'shard'))  38.6 us
    pallas_call x1, Pallas kernels, local(): pl.pallas_call(product_kernel, grid=(blocks,), out_shape=(jax.ShapeDtypeS...  31.5 us
    all_gather x1, waiting for transfers between devices, local(): inv_a = lax.all_gather(inv_a, 'shard', axis=0, tiled=True)  16.4 us
    broadcast_in_dim x1, other arithmetic, local(): return (precond * ascent_scale).astype(jnp.bfloat16)[None]  9.6 us
  transfers between devices with their start and end apart: 3, of which 3 were waited for; matrix products, arithmetic and copies ran while one was open for 0% of the time, Pallas kernels for 14%

profile of v2, /device:TPU:0, one launch (start us, length us, event | category | flops | bytes accessed | tf_op | source)
XLA Modules:
  0.0 371.0 jit_solution(4334765578300746740)
XLA Ops:
  6.5 0.9 copy.23
  7.7 0.2 select_reduce_fusion
  8.2 0.7 multiply_add_fusion
  9.0 0.3 convolution_convert_fusion.1
  9.4 0.2 copy.26
  9.6 0.4 reshape.55
  10.1 0.6 convolution_convert_fusion
  10.7 0.8 copy.27
  11.8 1.8 copy.25
  13.6 7.3 %all-to-all-start = ((bf16[32,20,1664]{2,1,0:T(8,128)(2,1)}), bf16[32,20,1664]{2,1,0:T(8,128)(2,1)S(1)}, u32[]{:S(2)}, u32[]{:S(2)}) async-start(bf16[32,20,1664]{2,1,0:T(8,128)(2,1)} %bitcast.20), calls=%async_computation | async-start | bytes 5111808 | tf_op jit(solution)/shard_map/all_to_all | solution.py:185
  21.0 59.9 %all-to-all-done = bf16[32,20,1664]{2,1,0:T(8,128)(2,1)S(1)} async-done(((bf16[32,20,1664]{2,1,0:T(8,128)(2,1)}), bf16[32,20,1664]{2,1,0:T(8,128)(2,1)S(1)}, u32[]{:S(2)}, u32[]{:S(2)}) %all-to-all-start) | async-done | bytes 2129952 | tf_op jit(solution)/shard_map/all_to_all | solution.py:185
  81.0 2.0 reshape.58
  82.9 1.7 convert_reduce_fusion
  84.6 1.1 slice.12.rows_ref
  85.8 40.0 %shard_map.55 = f32[2,256,256]{2,1,0:T(8,128)} custom-call(f32[2]{0:T(128)S(1)} %multiply_bitcast_fusion.1.damp_ref, f32[1]{0:T(128)} %bitcast.4.count_ref, bf16[640,512]{1,0:T(8,128)(2,1)S(1)} %slice.12.rows_ref), custom_call_target="tpu_custom_call" | custom-call | flops 20000000000 | bytes 4000000 | tf_op jit(solution)/shard_map/pallas_call | solution.py:134
  125.9 0.7 all-gather.6.cloned.1.call-update
  126.6 1.4 slice.14.rows_ref
  128.0 52.2 %shard_map.56 = (bf16[640,1024]{1,0:T(8,128)(2,1)S(1)}, bf16[640,1024]{1,0:T(8,128)(2,1)S(1)}) custom-call(f32[4]{0:T(128)S(1)} %multiply_bitcast_fusion.damp_ref, f32[1]{0:T(128)} %bitcast.4.count_ref, bf16[640,1024]{1,0:T(8,128)(2,1)S(1)} %slice.14.rows_ref), custom_call_target="tpu_custom_call" | custom-call | flops 20000000000 | bytes 4000000 | tf_op jit(solution)/shard_map/pallas_call | solution.py:134
  180.2 16.4 %all-gather.4.cloned.1.call-done.inv_ref = f32[16,256,256]{2,1,0:T(8,128)} async-done(((f32[2,256,256]{2,1,0:T(8,128)}), f32[16,256,256]{2,1,0:T(8,128)}) %all-gather.4.cloned.1.call-update) | async-done | bytes 4194320 | tf_op jit(solution)/shard_map/all_gather | solution.py:204
  196.6 86.6 %all-gather.6.cloned.1.call-done = bf16[5120,512]{1,0:T(8,128)(2,1)} async-done(((bf16[640,512]{1,0:T(8,128)(2,1)}), bf16[5120,512]{1,0:T(8,128)(2,1)}) %all-gather.6.cloned.1.call-update) | async-done | bytes 5242896 | tf_op jit(solution)/shard_map/all_gather | solution.py:191
  283.2 31.5 %shard_map.57 = (f32[4096,1024]{1,0:T(8,128)}, f32[8,1024]{1,0:T(8,128)S(1)}) custom-call(bf16[8,640,512]{2,1,0:T(8,128)(2,1)} %bitcast.25, f32[16,256,256]{2,1,0:T(8,128)} %all-gather.4.cloned.1.call-done.inv_ref, bf16[640,1024]{1,0:T(8,128)(2,1)S(1)} %get-tuple-element.9.high_ref, bf16[640,1024]{1,0:T(8,128)(2,1)S(1)} %get-tuple-element.10.low_ref), custom_call_target="tpu_custom_call" | custom-call | flops 16106127360 | bytes 16777216 | tf_op jit(solution)/shard_map/pallas_call | solution.py:211
  314.7 0.6 reduce_sum.58
  315.3 38.6 %psum.7 = f32[]{:T(128)} all-reduce(f32[]{:T(128)} %reduce_sum.58), channel_id=1, replica_groups=mesh['expert'=4,'shard'=8] {'expert','shard'}, use_global_device_ids=true, to_apply=%region_6.7 | all-reduce | flops 1 | bytes 8 | tf_op jit(solution)/shard_map/psum | solution.py:235
  354.6 9.6 %fusion = bf16[1,4096,1024]{2,1,0:T(8,128)(2,1)} fusion(f32[4096,1024]{1,0:T(8,128)} %get-tuple-element.11, f32[]{:T(128)S(6)} %rsqrt.3), kind=kLoop, calls=%fused_computation.2 | loop fusion | flops 8388608 | bytes 25165828 | tf_op jit(solution)/shard_map/broadcast_in_dim | solution.py:237
  (26 shorter events, 1.2 us)
Async XLA Ops:
  6.5 2.5 copy-start
  6.5 3.1 copy-start.2
  13.6 7.4 %copy-start.3 = (s32[1,16]{1,0:T(1,128)S(1)}, s32[1,16]{1,0:T(1,128)}, u32[]{:S(2)}) copy-start(s32[1,16]{1,0:T(1,128)} %param.8) | copy-start | bytes 196
  13.6 67.4 %all-to-all-start = ((bf16[32,20,1664]{2,1,0:T(8,128)(2,1)}), bf16[32,20,1664]{2,1,0:T(8,128)(2,1)S(1)}, u32[]{:S(2)}, u32[]{:S(2)}) async-start(bf16[32,20,1664]{2,1,0:T(8,128)(2,1)} %bitcast.20), calls=%async_computation | async-start | bytes 5111808 | tf_op jit(solution)/shard_map/all_to_all | solution.py:185
  20.9 175.7 %all-gather.4.cloned.1.call-start = ((), (), s32[]{:S(2)}) async-start(), calls=%async_computation.1 | async-start | bytes 4718592 | tf_op jit(solution)/shard_map/all_gather | solution.py:204
  85.7 40.1 %copy-start.1 = (bf16[640,512]{1,0:T(8,128)(2,1)}, bf16[640,512]{1,0:T(8,128)(2,1)S(1)}, u32[]{:S(2)}) copy-start(bf16[640,512]{1,0:T(8,128)(2,1)S(1)} %slice.12.rows_ref) | copy-start | bytes 1966084
  85.8 40.8 %copy-start.4 = (s32[1,4]{1,0:T(1,128)S(1)}, s32[1,4]{1,0:T(1,128)}, u32[]{:S(2)}) copy-start(s32[1,4]{1,0:T(1,128)} %param.9) | copy-start | bytes 52
  125.8 157.4 %all-gather.6.cloned.1.call-start = ((), (), s32[]{:S(2)}) async-start(), calls=%async_computation.2 | async-start | bytes 5898240 | tf_op jit(solution)/shard_map/all_gather | solution.py:191
Sparse Core Ops, SparseCore 0:
  126.0 70.5 all-gather.3
  198.7 84.4 all-gather.5
